TPU v7x, 32 devices: a whole 2x2x4 slice. The times are simulated.
32 devices in a mesh: seq: 8 (over y, x, core), mp: 4 (over z).
Axes of the slice: x: 2, y: 2, z: 4, core: 2. Of those that a mesh axis runs over, the one named last changes fastest.
Arguments:
- coarse: bfloat16 [768, 1024], P('mp', 'seq'), may hold values from -6 to 6
- skip: bfloat16 [768, 2048], P('mp', 'seq'), may hold values from -6 to 6
- conv_weight: bfloat16 [3, 768, 768], P(None, 'mp'), may hold values from -0.125 to 0.125
- conv_bias: float32 [768], P('mp'), may hold values from -3 to 3
- head_weight: bfloat16 [768, 512], P(None, 'mp'), may hold values from -0.21875 to 0.21875
- head_bias: float32 [512], P('mp'), may hold values from -3 to 3
- counts: int32 [2048, 512], P('seq', 'mp'), may hold values from 0 to 3
- seg_mask: int32 [1, 512], P(None, 'mp'), may hold values 0 or 1
Outputs:
- grad_skip: bfloat16 [768, 2048], P('mp', 'seq')
- grad_coarse: bfloat16 [768, 1024], P('mp', 'seq')
- grad_head: float32 [768, 512], P('seq', 'mp')
- grad_conv: float32 [768, 3, 768], P('seq', None, 'mp')
All inputs are finite; a program needn't handle non-finite values. No bound on the sum of `seg_mask` on one device may be relied on, other than what follows from the above.
Results may differ from a plain program's by a relative error of at most 0.0068.
Values may be sent and summed in bfloat16 or wider, within the bound.
No kernel may reach another device: no remote copies, remote signals or barrier semaphores. Data moves between devices by JAX's collectives and lax.ppermute only.
A program may use at most 64 MiB of HBM per device.

v0:
```python
import math
import jax
import jax.numpy as jnp
from jax import lax
from jax.sharding import PartitionSpec as P

root_two_pi = 0.7978845608028654
cubic_coef = 0.044715
multi_weight = 5.0
pseudo_count = 0.5


def extended(block, sides, width):
    for axis, dim in sides:
        count = lax.axis_size(axis)
        forward = [(i, i + 1) for i in range(count - 1)]
        backward = [(target, source) for source, target in forward]
        low = lax.ppermute(
            lax.slice_in_dim(block, block.shape[dim] - width, None, axis=dim), axis, forward
        )
        high = lax.ppermute(lax.slice_in_dim(block, 0, width, axis=dim), axis, backward)
        block = jnp.concatenate([low, block, high], axis=dim)
    return block


def gelu_value(inputs):
    inner = root_two_pi * (inputs + cubic_coef * inputs * inputs * inputs)
    return 0.5 * inputs * (1.0 + jnp.tanh(inner))


def gelu_slope(inputs):
    inner = root_two_pi * (inputs + cubic_coef * inputs * inputs * inputs)
    tangent = jnp.tanh(inner)
    return 0.5 * (1.0 + tangent) + 0.5 * inputs * (1.0 - tangent * tangent) * root_two_pi * (
        1.0 + 3.0 * cubic_coef * inputs * inputs
    )


def contract_first(left, right):
    return lax.dot_general(
        left, right, (((0,), (0,)), ((), ())), preferred_element_type=jnp.float32
    )


def contract_last(left, right):
    return lax.dot_general(
        left, right, (((1,), (1,)), ((), ())), preferred_element_type=jnp.float32
    )


def shards(coarse, skip, conv_weight, conv_bias, head_weight, head_bias, counts, seg_mask):
    width_dev = skip.shape[0]
    length_dev = skip.shape[1]
    taps = conv_weight.shape[0]
    reach = taps // 2
    seq_count = lax.axis_size("seq")
    scale_back = 1.0 / math.sqrt(length_dev * seq_count)
    doubled = jnp.repeat(coarse.astype(jnp.float32), 2, axis=1)
    summed = (doubled + skip.astype(jnp.float32)).astype(jnp.bfloat16)
    padded = extended(summed, (("seq", 1),), reach)
    widened = lax.all_gather(padded, "mp", axis=0, tiled=True)
    conv_out = jnp.zeros((width_dev, length_dev), jnp.float32)
    for offset in range(taps):
        conv_out = conv_out + jnp.dot(
            conv_weight[offset],
            widened[:, offset : offset + length_dev],
            preferred_element_type=jnp.float32,
        )
    before = conv_out + conv_bias[:, None]
    hidden = (summed.astype(jnp.float32) + gelu_value(before)).astype(jnp.bfloat16)
    hidden_full = lax.all_gather(hidden, "mp", axis=0, tiled=True)
    logits = contract_first(hidden_full, head_weight) + head_bias
    predicted = jax.nn.softplus(logits) + pseudo_count
    observed = counts.astype(jnp.float32)
    pred_sum = jnp.sum(predicted, axis=0)
    count_sum = jnp.sum(observed, axis=0)
    span = min(8, seq_count)
    position = lax.axis_index("seq")
    segment = position // span
    seg_count = seq_count // span
    member = (jnp.arange(seg_count, dtype=jnp.int32) == segment).astype(jnp.float32)[:, None]
    pred_table, count_table = lax.psum(
        (member * pred_sum[None, :], member * count_sum[None, :]), "seq"
    )
    pred_total = jnp.sum(member * pred_table, axis=0)
    count_total = jnp.sum(member * count_table, axis=0)
    mask_row = lax.dynamic_slice_in_dim(seg_mask, segment, 1, 0).astype(jnp.float32)
    slope_pred = mask_row * (
        1.0 + (multi_weight - 1.0) * count_total / pred_total - multi_weight * observed / predicted
    )
    grad_logits = (slope_pred * jax.nn.sigmoid(logits)).astype(jnp.bfloat16)
    track_full = lax.all_gather(grad_logits, "mp", axis=1, tiled=True)
    head_own = lax.all_to_all(head_weight, "mp", split_axis=0, concat_axis=1, tiled=True)
    grad_hidden = contract_last(head_own, track_full)
    grad_head = (
        lax.psum_scatter(
            jnp.dot(hidden_full, grad_logits, preferred_element_type=jnp.float32),
            "seq",
            scatter_dimension=0,
            tiled=True,
        )
        * scale_back
    )
    grad_before = (grad_hidden * gelu_slope(before)).astype(jnp.bfloat16)
    grad_padded = extended(grad_before, (("seq", 1),), reach)
    weight_rows = lax.all_to_all(conv_weight, "mp", split_axis=2, concat_axis=1, tiled=True)
    carry = jnp.zeros((width_dev, length_dev), jnp.float32)
    piece = lax.all_gather(grad_padded, "mp", axis=0, tiled=True)
    for offset in range(taps):
        first_row = 2 * reach - offset
        block = weight_rows[offset]
        carry = carry + contract_first(block, piece[:, first_row : first_row + length_dev])
    grad_input = grad_hidden + carry
    grad_skip = grad_input.astype(jnp.bfloat16)
    grad_coarse = jnp.sum(grad_input.reshape(width_dev, length_dev // 2, 2), axis=2).astype(
        jnp.bfloat16
    )
    grad_conv = (
        lax.psum_scatter(
            jnp.stack(
                [
                    contract_last(widened[:, offset : offset + length_dev], grad_before)
                    for offset in range(taps)
                ],
                axis=1,
            ),
            "seq",
            scatter_dimension=0,
            tiled=True,
        )
        * scale_back
    )
    return (grad_skip, grad_coarse, grad_head, grad_conv)


def solution(mesh):
    in_specs = (
        P("mp", "seq"),
        P("mp", "seq"),
        P(None, "mp", None),
        P("mp"),
        P(None, "mp"),
        P("mp"),
        P("seq", "mp"),
        P(None, "mp"),
    )
    out_specs = (P("mp", "seq"), P("mp", "seq"), P("seq", "mp"), P("seq", None, "mp"))
    return jax.shard_map(shards, mesh=mesh, in_specs=in_specs, out_specs=out_specs, check_vma=False)
```

profile of v0, /device:TPU:0, one launch (start us, length us, event | category | flops | bytes accessed | tf_op | source)
XLA Modules:
  0.0 156.0 jit_solution(14249767625792272399)
XLA Ops:
  7.2 0.9 copy.29
  8.1 0.1 broadcast_in_dim.2
  8.2 0.2 reshape.54
  8.4 0.1 copy.30
  8.5 0.9 add_convert_fusion.1
  9.4 0.1 fusion.34
  9.5 1.3 collective-permute-start.1
  10.8 3.0 %collective-permute-start = (bf16[192,1]{1,0:T(8,128)(2,1)S(1)}, bf16[192,1]{1,0:T(8,128)(2,1)S(1)}, u32[]{:S(2)}, u32[]{:S(2)}) collective-permute-start(bf16[192,1]{1,0:T(8,128)(2,1)S(1)} %get-tuple-element.27), channel_id=1, source_target_pairs={{0,4},{4,8},{8,12},{12,16},{16,20},{20,24},{24,28},{1,5},{5,9},{9,... | collective-permute-start | bytes 1160 | tf_op jit(solution)/shard_map/ppermute | solution.py:18
  13.9 6.4 %all-to-all-start = ((bf16[4,192,128]{2,1,0:T(8,128)(2,1)}), bf16[4,192,128]{2,1,0:T(8,128)(2,1)S(1)}, u32[]{:S(2)}, u32[]{:S(2)}) async-start(bf16[4,192,128]{2,1,0:T(8,128)(2,1)} %bitcast.9), calls=%async_computation | async-start | bytes 393216 | tf_op jit(solution)/shard_map/all_to_all | solution.py:93
  20.3 0.0 collective-permute-done.1
  20.3 0.1 maximum_bitcast_fusion
  20.5 0.1 copy.31
  20.6 18.7 %all-gather = bf16[4,192,258]{1,2,0:T(8,128)(2,1)S(1)} all-gather(bf16[1,192,258]{1,2,0:T(8,128)(2,1)S(1)} %copy.31), channel_id=1, replica_groups=mesh['seq'=8,'mp'=4] {'mp'}, dimensions={0}, use_global_device_ids=true | all-gather | bytes 495360 | tf_op jit(solution)/shard_map/all_gather | solution.py:61
  39.3 0.2 copy.32
  39.5 0.0 copy-start.2
  39.6 0.5 reshape.57
  40.1 0.3 fusion.13
  40.4 0.0 copy-start.4
  40.4 0.3 convolution_add_fusion.3
  40.7 0.4 add_convert_fusion
  41.1 15.0 %all_gather.13 = bf16[768,256]{1,0:T(8,128)(2,1)S(1)} all-gather(bf16[192,256]{1,0:T(8,128)(2,1)S(1)} %get-tuple-element.29), channel_id=1, replica_groups=mesh['seq'=8,'mp'=4] {'mp'}, dimensions={0}, use_global_device_ids=true | all-gather | bytes 491520 | tf_op jit(solution)/shard_map/all_gather | solution.py:71
  56.2 1.3 fusion.31
  57.5 11.8 %all-reduce = (f32[1,128]{1,0:T(1,128)S(1)}, f32[1,128]{1,0:T(1,128)S(1)}) all-reduce(f32[1,128]{1,0:T(1,128)S(1)} %get-tuple-element.37, f32[1,128]{1,0:T(1,128)S(1)} %get-tuple-element.38), channel_id=1, replica_groups=mesh['seq'=8,'mp'=4] {'seq'}, use_global_device_ids=true, to_apply=%region_3.4 | all-reduce | flops 256 | bytes 2048 | tf_op jit(solution)/shard_map/psum | solution.py:82
  69.3 0.1 multiply_convert_fusion
  69.4 1.0 fusion.36
  70.5 0.0 reduce-scatter.5.cloned.1.call-update
  70.5 0.0 reduce-scatter.7.cloned.1.call-start
  70.5 13.3 %all_gather.14 = bf16[256,512]{1,0:T(8,128)(2,1)S(1)} all-gather(bf16[256,128]{1,0:T(8,128)(2,1)S(1)} %multiply_convert_fusion), channel_id=1, replica_groups=mesh['seq'=8,'mp'=4] {'mp'}, dimensions={1}, use_global_device_ids=true | all-gather | bytes 327680 | tf_op jit(solution)/shard_map/all_gather | solution.py:92
  83.9 0.0 all-to-all-done
  83.9 0.3 fusion.27
  84.2 0.2 convolution_bitcast_fusion.2
  84.4 0.3 convolution_bitcast_fusion.1
  84.7 0.3 convolution_bitcast_fusion
  85.0 0.1 pad_maximum_fusion
  85.1 1.8 %copy.43 = f32[768,576]{1,0:T(8,128)} copy(f32[768,576]{0,1:T(8,128)S(1)} %bitcast.80) | data formatting | bytes 3538944
  86.9 0.0 reduce-scatter.7.cloned.1.call-update
  86.9 2.2 %copy.36 = bf16[3,192,768]{1,0,2:T(4,128)(2,1)} copy(bf16[3,192,768]{2,1,0:T(8,128)(2,1)S(1)} %copy-done) | data formatting | bytes 1769472 | tf_op args[2]
  89.1 3.6 %all-to-all-start.1 = ((bf16[3,192,768]{1,0,2:T(4,128)(2,1)}), bf16[3,192,768]{1,0,2:T(4,128)(2,1)S(1)}, u32[]{:S(2)}, u32[]{:S(2)}) async-start(bf16[3,192,768]{1,0,2:T(4,128)(2,1)} %copy.36), calls=%async_computation.1 | async-start | bytes 3145728 | tf_op jit(solution)/shard_map/all_to_all | solution.py:106
  92.7 0.1 fusion.33
  92.7 1.3 collective-permute-start.3
  94.0 3.0 %collective-permute-start.2 = (bf16[192,1]{1,0:T(8,128)(2,1)S(1)}, bf16[192,1]{1,0:T(8,128)(2,1)S(1)}, u32[]{:S(2)}, u32[]{:S(2)}) collective-permute-start(bf16[192,1]{1,0:T(8,128)(2,1)S(1)} %get-tuple-element.25), channel_id=1, source_target_pairs={{0,4},{4,8},{8,12},{12,16},{16,20},{20,24},{24,28},{1,5},{5,9},{9,... | collective-permute-start | bytes 1160 | tf_op jit(solution)/shard_map/ppermute | solution.py:18
  97.1 0.9 collective-permute-done.2
  97.9 0.1 maximum_bitcast_fusion.1
  98.1 0.1 copy.34
  98.2 39.4 %all-gather.1 = bf16[4,192,258]{1,2,0:T(8,128)(2,1)S(1)} all-gather(bf16[1,192,258]{1,2,0:T(8,128)(2,1)S(1)} %copy.34), channel_id=1, replica_groups=mesh['seq'=8,'mp'=4] {'mp'}, dimensions={0}, use_global_device_ids=true | all-gather | bytes 495360 | tf_op jit(solution)/shard_map/all_gather | solution.py:108
  137.6 0.2 copy.35
  137.8 0.5 reshape.59
  138.4 0.0 reduce-scatter.5.cloned.1.call-done
  138.4 1.4 broadcast_multiply_fusion.1
  139.8 1.1 copy.53
  140.9 0.4 fusion.32
  141.3 0.3 squeeze.21
  141.7 0.3 squeeze.22
  142.0 0.3 squeeze.23
  142.4 0.3 fusion.6
  142.7 0.3 convolution_add_fusion.1
  143.0 0.9 fusion.35
  144.0 0.1 copy.38
  144.1 0.1 reshape.55
  144.2 0.3 reduce_sum.29
  144.6 0.7 copy.39
  145.3 1.8 %reduce-scatter.7.cloned.1.call-done = f32[96,576]{1,0:T(8,128)} async-done(((f32[768,576]{1,0:T(8,128)}), f32[96,576]{1,0:T(8,128)}) %reduce-scatter.7.cloned.1.call-update) | async-done | bytes 221200
  147.2 1.1 copy.44
  148.3 0.9 copy.40
  (17 shorter events, 0.1 us)
Async XLA Ops:
  7.2 13.1 %copy-start.1 = (s32[256,128]{1,0:T(8,128)S(1)}, s32[256,128]{1,0:T(8,128)}, u32[]{:S(2)}) copy-start(s32[256,128]{1,0:T(8,128)} %param.14) | copy-start | bytes 393220
  7.2 13.1 %copy-start.3 = (s32[1,128]{1,0:T(1,128)S(1)}, s32[1,128]{1,0:T(1,128)}, u32[]{:S(2)}) copy-start(s32[1,128]{1,0:T(1,128)} %param.15) | copy-start | bytes 1540
  9.5 10.8 %collective-permute-start.1 = (bf16[192,1]{1,0:T(8,128)(2,1)S(1)}, bf16[192,1]{1,0:T(8,128)(2,1)S(1)}, u32[]{:S(2)}, u32[]{:S(2)}) collective-permute-start(bf16[192,1]{1,0:T(8,128)(2,1)S(1)} %get-tuple-element.28), channel_id=1, source_target_pairs={{4,0},{8,4},{12,8},{16,12},{20,16},{24,20},{28,24},{5,1},{9,5},{13... | collective-permute-start | bytes 1160 | tf_op jit(solution)/shard_map/ppermute | solution.py:21
  10.8 9.5 %collective-permute-start = (bf16[192,1]{1,0:T(8,128)(2,1)S(1)}, bf16[192,1]{1,0:T(8,128)(2,1)S(1)}, u32[]{:S(2)}, u32[]{:S(2)}) collective-permute-start(bf16[192,1]{1,0:T(8,128)(2,1)S(1)} %get-tuple-element.27), channel_id=1, source_target_pairs={{0,4},{4,8},{8,12},{12,16},{16,20},{20,24},{24,28},{1,5},{5,9},{9,... | collective-permute-start | bytes 1160 | tf_op jit(solution)/shard_map/ppermute | solution.py:18
  13.9 70.0 %all-to-all-start = ((bf16[4,192,128]{2,1,0:T(8,128)(2,1)}), bf16[4,192,128]{2,1,0:T(8,128)(2,1)S(1)}, u32[]{:S(2)}, u32[]{:S(2)}) async-start(bf16[4,192,128]{2,1,0:T(8,128)(2,1)} %bitcast.9), calls=%async_computation | async-start | bytes 393216 | tf_op jit(solution)/shard_map/all_to_all | solution.py:93
  20.2 19.9 %copy-start = (bf16[3,192,768]{2,1,0:T(8,128)(2,1)S(1)}, bf16[3,192,768]{2,1,0:T(8,128)(2,1)}, u32[]{:S(2)}) copy-start(bf16[3,192,768]{2,1,0:T(8,128)(2,1)} %param.10) | copy-start | bytes 2654212
  20.2 118.1 %reduce-scatter.5.cloned.1.call-start = ((), (), s32[]{:S(2)}) async-start(), calls=%async_computation.4 | async-start | bytes 442368 | tf_op jit(solution)/shard_map/reduce_scatter | solution.py:96
  39.5 1.2 copy-start.2
  40.4 15.7 %copy-start.4 = (f32[128]{0:T(128)S(1)}, f32[128]{0:T(128)}, u32[]{:S(2)}) copy-start(f32[128]{0:T(128)} %param.13) | copy-start | bytes 1540
  70.5 76.7 %reduce-scatter.7.cloned.1.call-start = ((), (), s32[]{:S(2)}) async-start(), calls=%async_computation.5 | async-start | bytes 2211840
  89.1 50.7 %all-to-all-start.1 = ((bf16[3,192,768]{1,0,2:T(4,128)(2,1)}), bf16[3,192,768]{1,0,2:T(4,128)(2,1)S(1)}, u32[]{:S(2)}, u32[]{:S(2)}) async-start(bf16[3,192,768]{1,0,2:T(4,128)(2,1)} %copy.36), calls=%async_computation.1 | async-start | bytes 3145728 | tf_op jit(solution)/shard_map/all_to_all | solution.py:106
  92.7 4.3 %collective-permute-start.3 = (bf16[192,1]{1,0:T(8,128)(2,1)S(1)}, bf16[192,1]{1,0:T(8,128)(2,1)S(1)}, u32[]{:S(2)}, u32[]{:S(2)}) collective-permute-start(bf16[192,1]{1,0:T(8,128)(2,1)S(1)} %get-tuple-element.26), channel_id=1, source_target_pairs={{4,0},{8,4},{12,8},{16,12},{20,16},{24,20},{28,24},{5,1},{9,5},{13... | collective-permute-start | bytes 1160 | tf_op jit(solution)/shard_map/ppermute | solution.py:21
  94.0 3.9 %collective-permute-start.2 = (bf16[192,1]{1,0:T(8,128)(2,1)S(1)}, bf16[192,1]{1,0:T(8,128)(2,1)S(1)}, u32[]{:S(2)}, u32[]{:S(2)}) collective-permute-start(bf16[192,1]{1,0:T(8,128)(2,1)S(1)} %get-tuple-element.25), channel_id=1, source_target_pairs={{0,4},{4,8},{8,12},{12,16},{16,20},{20,24},{24,28},{1,5},{5,9},{9,... | collective-permute-start | bytes 1160 | tf_op jit(solution)/shard_map/ppermute | solution.py:18
Sparse Core Ops, SparseCore 0:
  70.6 32.9 reduce-scatter.4
  107.0 40.1 reduce-scatter.6
where the time goes:
time: 157 us; the launch traced here: 156 us
  blocking collectives  98.3 us (63%)
  starting transfers between devices  18.6 us (12%)
  between operations  14.4 us (9%)
  local copies, waits for them, and re-layouts  12.7 us (8%)
  matrix products  5.91 us (4%)
  other arithmetic  3.27 us (2%)
  waiting for transfers between devices  2.76 us (2%)
    all_gather x1, blocking collectives, shards(): piece = lax.all_gather(grad_padded, 'mp', axis=0, tiled=True)  39.4 us
    all_gather x1, blocking collectives, shards(): widened = lax.all_gather(padded, 'mp', axis=0, tiled=True)  18.7 us
    all_gather x1, blocking collectives, shards(): hidden_full = lax.all_gather(hidden, 'mp', axis=0, tiled=True)  15 us
    all_gather x1, blocking collectives, shards(): track_full = lax.all_gather(grad_logits, 'mp', axis=1, tiled=True)  13.3 us
    psum x1, blocking collectives, shards(): lax.psum((member * pred_sum[None, :], member * count_sum[None, :]), 'seq')  11.8 us
    unnamed x19, local copies, waits for them, and re-layouts  8 us
    all_to_all x1, starting transfers between devices, shards(): lax.all_to_all(head_weight, 'mp', split_axis=0, concat_axis=1, tiled=True)  6.36 us
    ppermute x2, starting transfers between devices, extended(): lax.ppermute(lax.slice_in_dim(block, block.shape[dim] - width, None, axis...  6.07 us
  transfers between devices with their start and end apart: 8, of which 2 were waited for; matrix products, arithmetic and copies ran while one was open for 11% of the time, Pallas kernels for 0%

commit v1 on v0

--- a/solution.py
+++ b/solution.py
@@ -89,7 +89,7 @@
         1.0 + (multi_weight - 1.0) * count_total / pred_total - multi_weight * observed / predicted
     )
     grad_logits = (slope_pred * jax.nn.sigmoid(logits)).astype(jnp.bfloat16)
-    track_full = lax.all_gather(grad_logits, "mp", axis=1, tiled=True)
+    track_full = jnp.concatenate(lax.all_gather(grad_logits, "mp"), axis=1)
     head_own = lax.all_to_all(head_weight, "mp", split_axis=0, concat_axis=1, tiled=True)
     grad_hidden = contract_last(head_own, track_full)
     grad_head = (

time: 157 us -> 157 us (level)
  no operation moved by 1% of the time
where the time goes in v1:
time: 157 us; the launch traced here: 156 us
  blocking collectives  98.6 us (63%)
  starting transfers between devices  18.6 us (12%)
  between operations  14.4 us (9%)
  local copies, waits for them, and re-layouts  12.7 us (8%)
  matrix products  5.91 us (4%)
  other arithmetic  3.27 us (2%)
  waiting for transfers between devices  2.46 us (2%)
    all_gather x1, blocking collectives, shards(): piece = lax.all_gather(grad_padded, 'mp', axis=0, tiled=True)  38.8 us
    all_gather x1, blocking collectives, shards(): widened = lax.all_gather(padded, 'mp', axis=0, tiled=True)  18.7 us
    all_gather x1, blocking collectives, shards(): hidden_full = lax.all_gather(hidden, 'mp', axis=0, tiled=True)  15 us
    all_gather x1, blocking collectives, shards(): track_full = jnp.concatenate(lax.all_gather(grad_logits, 'mp'), axis=1)  14.3 us
    psum x1, blocking collectives, shards(): lax.psum((member * pred_sum[None, :], member * count_sum[None, :]), 'seq')  11.8 us
    unnamed x19, local copies, waits for them, and re-layouts  8 us
    all_to_all x1, starting transfers between devices, shards(): lax.all_to_all(head_weight, 'mp', split_axis=0, concat_axis=1, tiled=True)  6.36 us
    ppermute x2, starting transfers between devices, extended(): lax.ppermute(lax.slice_in_dim(block, block.shape[dim] - width, None, axis...  6.07 us
  transfers between devices with their start and end apart: 8, of which 2 were waited for; matrix products, arithmetic and copies ran while one was open for 11% of the time, Pallas kernels for 0%

profile of v1, /device:TPU:0, one launch (start us, length us, event | category | flops | bytes accessed | tf_op | source)
XLA Modules:
  0.0 156.0 jit_solution(9052603000118449284)
XLA Ops:
  7.2 0.9 copy.27
  8.1 0.1 broadcast_in_dim.2
  8.2 0.2 reshape.58
  8.4 0.1 copy.28
  8.5 0.9 add_convert_fusion.1
  9.4 0.1 fusion.33
  9.5 1.3 collective-permute-start.1
  10.8 3.0 %collective-permute-start = (bf16[192,1]{1,0:T(8,128)(2,1)S(1)}, bf16[192,1]{1,0:T(8,128)(2,1)S(1)}, u32[]{:S(2)}, u32[]{:S(2)}) collective-permute-start(bf16[192,1]{1,0:T(8,128)(2,1)S(1)} %get-tuple-element.27), channel_id=1, source_target_pairs={{0,4},{4,8},{8,12},{12,16},{16,20},{20,24},{24,28},{1,5},{5,9},{9,... | collective-permute-start | bytes 1160 | tf_op jit(solution)/shard_map/ppermute | solution.py:18
  13.9 6.4 %all-to-all-start = ((bf16[4,192,128]{2,1,0:T(8,128)(2,1)}), bf16[4,192,128]{2,1,0:T(8,128)(2,1)S(1)}, u32[]{:S(2)}, u32[]{:S(2)}) async-start(bf16[4,192,128]{2,1,0:T(8,128)(2,1)} %bitcast.11), calls=%async_computation | async-start | bytes 393216 | tf_op jit(solution)/shard_map/all_to_all | solution.py:93
  20.3 0.0 collective-permute-done.1
  20.3 0.1 maximum_bitcast_fusion
  20.5 0.1 copy.29
  20.6 18.7 %all-gather.1 = bf16[4,192,258]{1,2,0:T(8,128)(2,1)S(1)} all-gather(bf16[1,192,258]{1,2,0:T(8,128)(2,1)S(1)} %copy.29), channel_id=1, replica_groups=mesh['seq'=8,'mp'=4] {'mp'}, dimensions={0}, use_global_device_ids=true | all-gather | bytes 495360 | tf_op jit(solution)/shard_map/all_gather | solution.py:61
  39.3 0.2 copy.30
  39.5 0.0 copy-start.2
  39.6 0.5 reshape.63
  40.1 0.3 fusion.13
  40.4 0.0 copy-start.4
  40.4 0.3 convolution_add_fusion.3
  40.7 0.4 add_convert_fusion
  41.1 15.0 %all_gather.16 = bf16[768,256]{1,0:T(8,128)(2,1)S(1)} all-gather(bf16[192,256]{1,0:T(8,128)(2,1)S(1)} %get-tuple-element.29), channel_id=1, replica_groups=mesh['seq'=8,'mp'=4] {'mp'}, dimensions={0}, use_global_device_ids=true | all-gather | bytes 491520 | tf_op jit(solution)/shard_map/all_gather | solution.py:71
  56.2 1.3 fusion.30
  57.5 11.8 %all-reduce = (f32[1,128]{1,0:T(1,128)S(1)}, f32[1,128]{1,0:T(1,128)S(1)}) all-reduce(f32[1,128]{1,0:T(1,128)S(1)} %get-tuple-element.37, f32[1,128]{1,0:T(1,128)S(1)} %get-tuple-element.38), channel_id=1, replica_groups=mesh['seq'=8,'mp'=4] {'seq'}, use_global_device_ids=true, to_apply=%region_3.4 | all-reduce | flops 256 | bytes 2048 | tf_op jit(solution)/shard_map/psum | solution.py:82
  69.3 0.1 multiply_convert_fusion
  69.4 1.0 fusion.35
  70.5 0.0 reduce-scatter.5.cloned.1.call-update
  70.5 0.0 reduce-scatter.7.cloned.1.call-start
  70.5 14.3 %all-gather = bf16[1024,128]{1,0:T(8,128)(2,1)S(1)} all-gather(bf16[256,128]{1,0:T(8,128)(2,1)S(1)} %multiply_convert_fusion), channel_id=2, replica_groups=mesh['seq'=8,'mp'=4] {'mp'}, dimensions={0}, use_global_device_ids=true | all-gather | bytes 327680 | tf_op jit(solution)/shard_map/all_gather | solution.py:92
  84.8 0.0 all-to-all-done
  84.8 0.3 fusion.27
  85.1 0.2 convolution_bitcast_fusion.2
  85.3 0.3 convolution_bitcast_fusion.1
  85.6 0.3 convolution_bitcast_fusion
  85.9 0.1 pad_maximum_fusion
  86.0 1.8 %copy.40 = f32[768,576]{1,0:T(8,128)} copy(f32[768,576]{0,1:T(8,128)S(1)} %bitcast.80) | data formatting | bytes 3538944
  87.8 0.0 reduce-scatter.7.cloned.1.call-update
  87.9 2.2 %copy.33 = bf16[3,192,768]{1,0,2:T(4,128)(2,1)} copy(bf16[3,192,768]{2,1,0:T(8,128)(2,1)S(1)} %copy-done) | data formatting | bytes 1769472 | tf_op args[2]
  90.0 3.6 %all-to-all-start.1 = ((bf16[3,192,768]{1,0,2:T(4,128)(2,1)}), bf16[3,192,768]{1,0,2:T(4,128)(2,1)S(1)}, u32[]{:S(2)}, u32[]{:S(2)}) async-start(bf16[3,192,768]{1,0,2:T(4,128)(2,1)} %copy.33), calls=%async_computation.1 | async-start | bytes 3145728 | tf_op jit(solution)/shard_map/all_to_all | solution.py:106
  93.6 0.1 fusion.32
  93.7 1.3 collective-permute-start.3
  95.0 3.0 %collective-permute-start.2 = (bf16[192,1]{1,0:T(8,128)(2,1)S(1)}, bf16[192,1]{1,0:T(8,128)(2,1)S(1)}, u32[]{:S(2)}, u32[]{:S(2)}) collective-permute-start(bf16[192,1]{1,0:T(8,128)(2,1)S(1)} %get-tuple-element.25), channel_id=1, source_target_pairs={{0,4},{4,8},{8,12},{12,16},{16,20},{20,24},{24,28},{1,5},{5,9},{9,... | collective-permute-start | bytes 1160 | tf_op jit(solution)/shard_map/ppermute | solution.py:18
  98.0 0.9 collective-permute-done.2
  98.9 0.1 maximum_bitcast_fusion.1
  99.0 0.1 copy.31
  99.1 38.8 %all-gather.2 = bf16[4,192,258]{1,2,0:T(8,128)(2,1)S(1)} all-gather(bf16[1,192,258]{1,2,0:T(8,128)(2,1)S(1)} %copy.31), channel_id=1, replica_groups=mesh['seq'=8,'mp'=4] {'mp'}, dimensions={0}, use_global_device_ids=true | all-gather | bytes 495360 | tf_op jit(solution)/shard_map/all_gather | solution.py:108
  137.9 0.2 copy.32
  138.1 0.5 reshape.65
  138.7 0.0 reduce-scatter.5.cloned.1.call-done
  138.7 1.4 broadcast_multiply_fusion.1
  140.1 1.1 copy.43
  141.2 0.4 fusion.31
  141.6 0.3 squeeze.21
  142.0 0.3 squeeze.22
  142.3 0.3 squeeze.23
  142.7 0.3 fusion.6
  143.0 0.3 convolution_add_fusion.1
  143.3 0.9 fusion.34
  144.3 0.1 copy.35
  144.4 0.1 reshape.60
  144.6 0.3 reduce_sum.29
  144.9 0.7 copy.36
  145.6 1.5 reduce-scatter.7.cloned.1.call-done
  147.2 1.1 copy.41
  148.3 0.9 copy.37
  (17 shorter events, 0.1 us)
Async XLA Ops:
  7.2 13.1 %copy-start.1 = (s32[256,128]{1,0:T(8,128)S(1)}, s32[256,128]{1,0:T(8,128)}, u32[]{:S(2)}) copy-start(s32[256,128]{1,0:T(8,128)} %param.14) | copy-start | bytes 393220
  7.2 13.1 %copy-start.3 = (s32[1,128]{1,0:T(1,128)S(1)}, s32[1,128]{1,0:T(1,128)}, u32[]{:S(2)}) copy-start(s32[1,128]{1,0:T(1,128)} %param.15) | copy-start | bytes 1540
  9.5 10.8 %collective-permute-start.1 = (bf16[192,1]{1,0:T(8,128)(2,1)S(1)}, bf16[192,1]{1,0:T(8,128)(2,1)S(1)}, u32[]{:S(2)}, u32[]{:S(2)}) collective-permute-start(bf16[192,1]{1,0:T(8,128)(2,1)S(1)} %get-tuple-element.28), channel_id=1, source_target_pairs={{4,0},{8,4},{12,8},{16,12},{20,16},{24,20},{28,24},{5,1},{9,5},{13... | collective-permute-start | bytes 1160 | tf_op jit(solution)/shard_map/ppermute | solution.py:21
  10.8 9.5 %collective-permute-start = (bf16[192,1]{1,0:T(8,128)(2,1)S(1)}, bf16[192,1]{1,0:T(8,128)(2,1)S(1)}, u32[]{:S(2)}, u32[]{:S(2)}) collective-permute-start(bf16[192,1]{1,0:T(8,128)(2,1)S(1)} %get-tuple-element.27), channel_id=1, source_target_pairs={{0,4},{4,8},{8,12},{12,16},{16,20},{20,24},{24,28},{1,5},{5,9},{9,... | collective-permute-start | bytes 1160 | tf_op jit(solution)/shard_map/ppermute | solution.py:18
  13.9 70.9 %all-to-all-start = ((bf16[4,192,128]{2,1,0:T(8,128)(2,1)}), bf16[4,192,128]{2,1,0:T(8,128)(2,1)S(1)}, u32[]{:S(2)}, u32[]{:S(2)}) async-start(bf16[4,192,128]{2,1,0:T(8,128)(2,1)} %bitcast.11), calls=%async_computation | async-start | bytes 393216 | tf_op jit(solution)/shard_map/all_to_all | solution.py:93
  20.2 19.9 %copy-start = (bf16[3,192,768]{2,1,0:T(8,128)(2,1)S(1)}, bf16[3,192,768]{2,1,0:T(8,128)(2,1)}, u32[]{:S(2)}) copy-start(bf16[3,192,768]{2,1,0:T(8,128)(2,1)} %param.10) | copy-start | bytes 2654212
  20.2 118.4 %reduce-scatter.5.cloned.1.call-start = ((), (), s32[]{:S(2)}) async-start(), calls=%async_computation.4 | async-start | bytes 442368 | tf_op jit(solution)/shard_map/reduce_scatter | solution.py:96
  39.5 1.2 copy-start.2
  40.4 15.7 %copy-start.4 = (f32[128]{0:T(128)S(1)}, f32[128]{0:T(128)}, u32[]{:S(2)}) copy-start(f32[128]{0:T(128)} %param.13) | copy-start | bytes 1540
  70.5 76.7 %reduce-scatter.7.cloned.1.call-start = ((), (), s32[]{:S(2)}) async-start(), calls=%async_computation.5 | async-start | bytes 2211840
  90.0 50.1 %all-to-all-start.1 = ((bf16[3,192,768]{1,0,2:T(4,128)(2,1)}), bf16[3,192,768]{1,0,2:T(4,128)(2,1)S(1)}, u32[]{:S(2)}, u32[]{:S(2)}) async-start(bf16[3,192,768]{1,0,2:T(4,128)(2,1)} %copy.33), calls=%async_computation.1 | async-start | bytes 3145728 | tf_op jit(solution)/shard_map/all_to_all | solution.py:106
  93.7 4.3 %collective-permute-start.3 = (bf16[192,1]{1,0:T(8,128)(2,1)S(1)}, bf16[192,1]{1,0:T(8,128)(2,1)S(1)}, u32[]{:S(2)}, u32[]{:S(2)}) collective-permute-start(bf16[192,1]{1,0:T(8,128)(2,1)S(1)} %get-tuple-element.26), channel_id=1, source_target_pairs={{4,0},{8,4},{12,8},{16,12},{20,16},{24,20},{28,24},{5,1},{9,5},{13... | collective-permute-start | bytes 1160 | tf_op jit(solution)/shard_map/ppermute | solution.py:21
  95.0 3.9 %collective-permute-start.2 = (bf16[192,1]{1,0:T(8,128)(2,1)S(1)}, bf16[192,1]{1,0:T(8,128)(2,1)S(1)}, u32[]{:S(2)}, u32[]{:S(2)}) collective-permute-start(bf16[192,1]{1,0:T(8,128)(2,1)S(1)} %get-tuple-element.25), channel_id=1, source_target_pairs={{0,4},{4,8},{8,12},{12,16},{16,20},{20,24},{24,28},{1,5},{5,9},{9,... | collective-permute-start | bytes 1160 | tf_op jit(solution)/shard_map/ppermute | solution.py:18
Sparse Core Ops, SparseCore 0:
  70.6 32.9 reduce-scatter.4
  107.0 40.0 reduce-scatter.6
